TPU v7x, 32 devices: a whole 2x2x4 slice. The times are simulated.
32 devices in a mesh: tm: 2 (over core), lat: 16 (over z, y, x).
Axes of the slice: x: 2, y: 2, z: 4, core: 2. Of those that a mesh axis runs over, the one named last changes fastest.
Arguments:
- spectral_state: float32 [4, 16, 2, 16, 256], P('tm', 'lat'), may hold values from -6 to 6
- legendre: bfloat16 [16, 16, 16], P('lat'), may hold values from -1.5 to 1.5
- wave_slots: int32 [16], replicated, may hold values from 0 to 15, each once
- lat_order: int32 [16], replicated, may hold values from 0 to 15, each once
- quad_weights: float32 [16], replicated, may hold values from 0.2 to 1
- available: int32 [4, 8, 16, 256], P('tm', None, 'lat'), may hold values 0 or 1
- targets: float32 [4, 4, 8], P('tm'), may hold values from -6 to 6
- w_first: float32 [256, 384], replicated, may hold values from -0.375 to 0.375
- w_mid: float32 [384, 384], replicated, may hold values from -0.3125 to 0.3125
- w_last: float32 [384, 256], replicated, may hold values from -0.3125 to 0.3125
- norm_bias: float32 [2, 1024], replicated, may hold values from -0.3 to 0.3
- mean_first: float32 [256, 384], replicated, may hold values from -0.00061035156 to 0.00061035156
- mean_mid: float32 [384, 384], replicated, may hold values from -0.00061035156 to 0.00061035156
- mean_last: float32 [384, 256], replicated, may hold values from -0.00061035156 to 0.00061035156
- mean_bias: float32 [2, 1024], replicated, may hold values from -0.00061035156 to 0.00061035156
- square_first: float32 [256, 384], replicated, may hold values from 3e-10 to 3e-08
- square_mid: float32 [384, 384], replicated, may hold values from 3e-10 to 3e-08
- square_last: float32 [384, 256], replicated, may hold values from 3e-10 to 3e-08
- square_bias: float32 [2, 1024], replicated, may hold values from 3e-10 to 3e-08
Outputs:
- loss: float32 [], replicated
- grad_norm: float32 [], replicated
- master_first: float32 [256, 384], replicated
- master_mid: float32 [384, 384], replicated
- master_last: float32 [384, 256], replicated
- master_bias: float32 [2, 1024], replicated
- new_mean_first: float32 [256, 384], replicated
- new_mean_mid: float32 [384, 384], replicated
- new_mean_last: float32 [384, 256], replicated
- new_mean_bias: float32 [2, 1024], replicated
- new_square_first: float32 [256, 384], replicated
- new_square_mid: float32 [384, 384], replicated
- new_square_last: float32 [384, 256], replicated
- new_square_bias: float32 [2, 1024], replicated
- half_first: bfloat16 [256, 384], replicated
- half_mid: bfloat16 [384, 384], replicated
- half_last: bfloat16 [384, 256], replicated
- half_bias: bfloat16 [2, 1024], replicated
Inputs may be any that keep to these rules, and one draw needn't show every extreme that they name: `wave_slots`: each wavenumber 0 to 15 stands in one slot; slot j lies on the device of index j // 1 of lat. `lat_order`: each latitude stands in one grid row.
All inputs are finite; a program needn't handle non-finite values. No bound on the sum of `available` on one device may be relied on, other than what follows from the above.
Results may differ from a plain program's by a relative error of at most 0.0082.
Values may be sent and summed in bfloat16 or wider, within the bound.
No kernel may reach another device: no remote copies, remote signals or barrier semaphores. Data moves between devices by JAX's collectives and lax.ppermute only.
A program may use at most 128 MiB of HBM per device.

v0:
```python
from functools import partial
import math
import jax
import jax.numpy as jnp
from jax import lax
from jax.sharding import PartitionSpec as P

STEPS = 4
EPS_NORM = 1e-05
STEP_SCALE = 0.5
CLIP_NORM = 1.0
LEARN_RATE = 0.01
BETA_ONE = 0.9
BETA_TWO = 0.95
EPS_ADAM = 1e-08
DECAY = 0.1
HIGH = lax.Precision.HIGHEST


def wave_tables(wave_slots, lon_count):
    product = wave_slots[:, None] * jnp.arange(lon_count, dtype=jnp.int32)[None, :] % lon_count
    phase = product.astype(jnp.float32) * (2.0 * math.pi / lon_count)
    inverse = jnp.stack([jnp.cos(phase), -jnp.sin(phase)], axis=1)
    scale = jnp.where(wave_slots == 0, 1.0, 2.0).astype(jnp.float32) / lon_count
    return (inverse.astype(jnp.bfloat16), (inverse * scale[:, None, None]).astype(jnp.bfloat16))


def layer_spans(chans, hidden):
    gains = [(0, chans), (chans, hidden), (chans + hidden, hidden)]
    biases = [(0, hidden), (hidden, hidden), (2 * hidden, chans)]
    return list(zip(gains, biases))


def norm_gain(x, gain):
    centre = x - jnp.mean(x, axis=-1, keepdims=True)
    return centre * lax.rsqrt(jnp.mean(centre * centre, axis=-1, keepdims=True) + EPS_NORM) * gain


def corrector_forward(x, weights, norm_bias):
    spans = layer_spans(weights[0].shape[0], weights[0].shape[1])
    saved = []
    for k in range(3):
        (gstart, gwidth), (bstart, bwidth) = spans[k]
        h_low = norm_gain(x, 1.0 + norm_bias[0, gstart : gstart + gwidth]).astype(jnp.bfloat16)
        z_val = (
            jnp.dot(h_low, weights[k], preferred_element_type=jnp.float32)
            + norm_bias[1, bstart : bstart + bwidth]
        )
        saved.append((x, h_low, z_val))
        x = jax.nn.gelu(z_val, approximate=False) if k < 2 else z_val
    return (x, saved)


def corrector_backward(grad, saved, weights, norm_bias):
    spans = layer_spans(weights[0].shape[0], weights[0].shape[1])
    weight_grads = [None, None, None]
    gain_parts = [None, None, None]
    bias_parts = [None, None, None]
    for k in (2, 1, 0):
        (gstart, gwidth), (bstart, bwidth) = spans[k]
        x, h_low, z_val = saved[k]
        if k < 2:
            grad = jax.vjp(partial(jax.nn.gelu, approximate=False), z_val)[1](grad)[0]
        grad_low = grad.astype(jnp.bfloat16)
        weight_grads[k] = lax.dot_general(
            h_low, grad_low, (((0,), (0,)), ((), ())), preferred_element_type=jnp.float32
        )
        bias_parts[k] = jnp.sum(grad_low, axis=0, dtype=jnp.float32)
        back_h = lax.dot_general(
            grad_low, weights[k], (((1,), (1,)), ((), ())), preferred_element_type=jnp.float32
        )
        grad, gain_parts[k] = jax.vjp(norm_gain, x, 1.0 + norm_bias[0, gstart : gstart + gwidth])[
            1
        ](back_h)
    vector_grad = jnp.stack([jnp.concatenate(gain_parts), jnp.concatenate(bias_parts)])
    return (grad, (weight_grads[0], weight_grads[1], weight_grads[2], vector_grad))


def adamw(weight, mean, square, grad):
    mean_new = BETA_ONE * mean + (1.0 - BETA_ONE) * grad
    square_new = BETA_TWO * square + (1.0 - BETA_TWO) * grad * grad
    weight_new = weight - LEARN_RATE * (
        mean_new / (jnp.sqrt(square_new) + EPS_ADAM) + DECAY * weight
    )
    return (weight_new, mean_new, square_new)


def per_device(
    spectral_state,
    legendre,
    wave_slots,
    lat_order,
    quad_weights,
    available,
    targets,
    w_first,
    w_mid,
    w_last,
    norm_bias,
    mean_first,
    mean_mid,
    mean_last,
    mean_bias,
    square_first,
    square_mid,
    square_last,
    square_bias,
):
    tdev, wdev, _, degrees, chans = spectral_state.shape
    fields = available.shape[1]
    rows_dev = available.shape[2]
    lon_count = available.shape[3]
    levels = chans // fields
    lat_index = lax.axis_index("lat")
    slots = lax.dynamic_slice_in_dim(wave_slots, lat_index * wdev, wdev)
    finv, ffw = wave_tables(wave_slots, lon_count)
    keep = (jnp.arange(degrees, dtype=jnp.int32)[None, :] >= slots[:, None]).astype(jnp.bfloat16)
    plg = jnp.take(legendre, lat_order, axis=2) * keep[:, :, None]
    qrow = jnp.take(quad_weights, lat_order)
    qlocal = lax.dynamic_slice_in_dim(qrow, lat_index * rows_dev, rows_dev)
    colw = qlocal[None, None, :, None] * available.astype(jnp.float32)
    den_part = jnp.sum(colw, axis=(2, 3))
    params = (w_first, w_mid, w_last, norm_bias)
    weights = (
        w_first.astype(jnp.bfloat16),
        w_mid.astype(jnp.bfloat16),
        w_last.astype(jnp.bfloat16),
    )

    def legendre_sum(piece):
        return jnp.einsum("mnr,tmprc->tmpnc", plg, piece, preferred_element_type=jnp.float32)

    def fourier_sum(table, piece):
        return jnp.einsum("mpk,tmprc->trkc", table, piece, preferred_element_type=jnp.float32)

    def to_grid(state):
        sums = jnp.einsum(
            "mnr,tmpnc->tmprc", plg, state.astype(jnp.bfloat16), preferred_element_type=jnp.float32
        ).astype(jnp.bfloat16)
        return fourier_sum(
            finv, lax.all_to_all(sums, "lat", split_axis=3, concat_axis=1, tiled=True)
        )

    def column_pass(grid):
        out, saved = corrector_forward(grid.reshape(-1, chans), weights, norm_bias)
        return (out.reshape(grid.shape), saved)

    states = []
    nums = []
    den_total = den_part
    state = spectral_state
    for s in range(STEPS):
        states.append(state)
        grid = to_grid(state)
        out, saved = column_pass(grid)
        pred = grid + STEP_SCALE * out
        num_part = jnp.einsum(
            "tfrk,trkfl->tf",
            colw,
            pred.reshape(tdev, rows_dev, lon_count, fields, levels),
            precision=HIGH,
        )
        num_total, den_total = lax.psum((num_part, den_part), "lat")
        nums.append(num_total)
        tend = (out * qlocal[None, :, None, None]).astype(jnp.bfloat16)
        coeff = jnp.einsum("mpk,trkc->tmprc", ffw, tend, preferred_element_type=jnp.float32).astype(
            jnp.bfloat16
        )
        spec = legendre_sum(lax.all_to_all(coeff, "lat", split_axis=1, concat_axis=3, tiled=True))
        state = state + STEP_SCALE * spec
    num_all = jnp.stack(nums)
    bias = num_all / (levels * den_total[None]) - jnp.moveaxis(targets, 1, 0)
    loss = lax.psum(jnp.sum(bias * bias) / STEPS, "tm")
    grad_bias = 2.0 * bias / (STEPS * levels * den_total[None])
    totals = tuple((jnp.zeros_like(p) for p in params))
    back_state = None
    for s in reversed(range(STEPS)):
        grid = to_grid(states[s])
        out, saved = column_pass(grid)
        scaled = jnp.moveaxis(colw * grad_bias[s][:, :, None, None], 1, 3)
        back_pred = jnp.broadcast_to(scaled[..., None], scaled.shape + (levels,)).reshape(
            grid.shape
        )
        back_out = STEP_SCALE * back_pred
        if back_state is not None:
            back_spec = (STEP_SCALE * back_state).astype(jnp.bfloat16)
            back_coeff = jnp.einsum(
                "mnr,tmpnc->tmprc", plg, back_spec, preferred_element_type=jnp.float32
            ).astype(jnp.bfloat16)
            back_tend = fourier_sum(
                ffw, lax.all_to_all(back_coeff, "lat", split_axis=3, concat_axis=1, tiled=True)
            )
            back_out = back_out + qlocal[None, :, None, None] * back_tend
        back_in, grads = corrector_backward(back_out.reshape(-1, chans), saved, weights, norm_bias)
        totals = tuple((a + b for a, b in zip(totals, grads)))
        if s > 0:
            back_grid = (back_pred + back_in.reshape(grid.shape)).astype(jnp.bfloat16)
            back_sums = jnp.einsum(
                "mpk,trkc->tmprc", finv, back_grid, preferred_element_type=jnp.float32
            ).astype(jnp.bfloat16)
            back_low = legendre_sum(
                lax.all_to_all(back_sums, "lat", split_axis=1, concat_axis=3, tiled=True)
            )
            back_state = back_low if back_state is None else back_state + back_low
    means = (mean_first, mean_mid, mean_last, mean_bias)
    squares = (square_first, square_mid, square_last, square_bias)
    grads = lax.psum(totals, ("tm", "lat"))
    grad_norm = jnp.sqrt(sum((jnp.sum(g * g) for g in grads)))
    factor = CLIP_NORM / jnp.maximum(grad_norm, CLIP_NORM)
    results = [adamw(w, a, b, g * factor) for w, a, b, g in zip(params, means, squares, grads)]
    masters = [r[0] for r in results]
    new_means = [r[1] for r in results]
    new_squares = [r[2] for r in results]
    halves = [w.astype(jnp.bfloat16) for w in masters]
    return (
        loss,
        grad_norm,
        masters[0],
        masters[1],
        masters[2],
        masters[3],
        new_means[0],
        new_means[1],
        new_means[2],
        new_means[3],
        new_squares[0],
        new_squares[1],
        new_squares[2],
        new_squares[3],
        halves[0],
        halves[1],
        halves[2],
        halves[3],
    )


def solution(mesh):
    in_specs = (
        P("tm", "lat", None, None, None),
        P("lat", None, None),
        P(),
        P(),
        P(),
        P("tm", None, "lat", None),
        P("tm", None, None),
        P(),
        P(),
        P(),
        P(),
        P(),
        P(),
        P(),
        P(),
        P(),
        P(),
        P(),
        P(),
    )
    out_specs = (
        P(),
        P(),
        P(),
        P(),
        P(),
        P(),
        P(),
        P(),
        P(),
        P(),
        P(),
        P(),
        P(),
        P(),
        P(),
        P(),
        P(),
        P(),
    )
    return jax.shard_map(
        per_device, mesh=mesh, in_specs=in_specs, out_specs=out_specs, check_vma=False
    )
```

profile of v0, /device:TPU:0, one launch (start us, length us, event | category | flops | bytes accessed | tf_op | source)
XLA Modules:
  0.0 490.8 jit_solution(849199737556524078)
XLA Ops:
  11.4 8.3 %all-to-all-start = ((bf16[2,1,2,16,256]{4,2,0,1,3:T(2,128)(2,1)}), bf16[2,1,2,16,256]{4,2,0,1,3:T(2,128)(2,1)S(1)}, u32[]{:S(2)}, u32[]{:S(2)}) async-start(bf16[2,1,2,16,256]{4,2,0,1,3:T(2,128)(2,1)} %copy.194), calls=%async_computation | async-start | bytes 65536 | tf_op jit(solution)/shard_map/all_to_all | solution.py:141
  21.9 5.3 %all-to-all-done = bf16[2,1,2,16,256]{4,2,0,1,3:T(2,128)(2,1)S(1)} async-done(((bf16[2,1,2,16,256]{4,2,0,1,3:T(2,128)(2,1)}), bf16[2,1,2,16,256]{4,2,0,1,3:T(2,128)(2,1)S(1)}, u32[]{:S(2)}, u32[]{:S(2)}) %all-to-all-start) | async-done | bytes 32800 | tf_op jit(solution)/shard_map/all_to_all | solution.py:141
  28.0 3.0 fusion.214
  31.9 3.2 fusion.212
  37.8 10.0 %all_to_all.215 = bf16[2,16,2,1,256]{4,2,0,3,1:T(2,128)(2,1)S(1)} all-to-all(bf16[2,16,2,1,256]{4,2,0,3,1:T(2,128)(2,1)S(1)} %copy.198), channel_id=1, replica_groups=mesh['tm'=2,'lat'=16] {'lat'}, dimensions={1} | all-to-all | bytes 65536 | tf_op jit(solution)/shard_map/all_to_all | solution.py:169
  48.2 10.1 %all_to_all.216 = bf16[2,1,2,16,256]{4,2,0,1,3:T(2,128)(2,1)S(1)} all-to-all(bf16[2,1,2,16,256]{4,2,0,1,3:T(2,128)(2,1)S(1)} %copy.202), channel_id=1, replica_groups=mesh['tm'=2,'lat'=16] {'lat'}, dimensions={3} | all-to-all | bytes 65536 | tf_op jit(solution)/shard_map/all_to_all | solution.py:141
  60.6 3.0 fusion.210
  64.5 3.2 fusion.208
  70.5 10.0 %all_to_all.217 = bf16[2,16,2,1,256]{4,2,0,3,1:T(2,128)(2,1)S(1)} all-to-all(bf16[2,16,2,1,256]{4,2,0,3,1:T(2,128)(2,1)S(1)} %copy.206), channel_id=1, replica_groups=mesh['tm'=2,'lat'=16] {'lat'}, dimensions={1} | all-to-all | bytes 65536 | tf_op jit(solution)/shard_map/all_to_all | solution.py:169
  80.8 10.0 %all_to_all.218 = bf16[2,1,2,16,256]{4,2,0,1,3:T(2,128)(2,1)S(1)} all-to-all(bf16[2,1,2,16,256]{4,2,0,1,3:T(2,128)(2,1)S(1)} %copy.209), channel_id=1, replica_groups=mesh['tm'=2,'lat'=16] {'lat'}, dimensions={3} | all-to-all | bytes 65536 | tf_op jit(solution)/shard_map/all_to_all | solution.py:141
  93.4 3.1 fusion.206
  96.7 3.2 fusion.204
  100.0 1.9 broadcast_multiply_fusion
  102.1 10.0 %all_to_all.219 = bf16[2,16,2,1,256]{4,2,0,3,1:T(2,128)(2,1)S(1)} all-to-all(bf16[2,16,2,1,256]{4,2,0,3,1:T(2,128)(2,1)S(1)} %copy.213), channel_id=1, replica_groups=mesh['tm'=2,'lat'=16] {'lat'}, dimensions={1} | all-to-all | bytes 65536 | tf_op jit(solution)/shard_map/all_to_all | solution.py:169
  113.0 3.8 all-to-all-start.6
  117.7 2.0 copy.197
  122.8 2.1 copy.205
  124.9 1.9 add.549
  127.9 2.1 copy.212
  130.0 1.9 add.558
  136.3 3.1 fusion.202
  140.6 3.2 fusion.200
  145.1 2.1 copy.219
  147.2 2.1 add.567
  150.4 42.5 %all-reduce.1 = (f32[1,2,8]{2,1,0:T(2,128)S(1)}, f32[1,2,8]{2,1,0:T(2,128)S(1)}, f32[1,2,8]{2,1,0:T(2,128)S(1)}, f32[1,2,8]{2,1,0:T(2,128)S(1)}, f32[2,8]{1,0:T(2,128)S(1)}) all-reduce(f32[1,2,8]{2,1,0:T(2,128)S(1)} %bitcast.673, f32[1,2,8]{2,1,0:T(2,128)S(1)} %bitcast.674, ...), channel_id=1, replica_groups=mesh['tm'=2,'lat'=16] {'lat'}, use_global_device_ids=true, to_apply=%region_31.32 | all-reduce | flops 80 | bytes 640 | tf_op jit(solution)/shard_map/psum | solution.py:163
  203.2 1.9 convert_reduce_fusion.7
  205.1 2.8 multiply_reduce_fusion.27
  208.6 2.2 fusion.220
  210.8 3.4 psum.75
  218.5 2.0 copy.233
  221.4 2.0 copy.253
  224.2 2.0 copy.243
  230.8 3.6 all-to-all-start.7
  235.2 6.7 %all-to-all-done.7 = bf16[2,16,2,1,256]{4,2,0,3,1:T(2,128)(2,1)S(1)} async-done(((bf16[2,16,2,1,256]{4,2,0,3,1:T(2,128)(2,1)}), bf16[2,16,2,1,256]{4,2,0,3,1:T(2,128)(2,1)S(1)}, u32[]{:S(2)}, u32[]{:S(2)}) %all-to-all-start.7) | async-done | bytes 32800 | tf_op jit(solution)/shard_map/all_to_all | solution.py:202
  242.8 3.5 all-to-all-start.8
  247.0 6.6 %all-to-all-done.8 = bf16[2,1,2,16,256]{4,2,0,1,3:T(2,128)(2,1)S(1)} async-done(((bf16[2,1,2,16,256]{4,2,0,1,3:T(2,128)(2,1)}), bf16[2,1,2,16,256]{4,2,0,1,3:T(2,128)(2,1)S(1)}, u32[]{:S(2)}, u32[]{:S(2)}) %all-to-all-start.8) | async-done | bytes 32800 | tf_op jit(solution)/shard_map/all_to_all | solution.py:191
  253.7 2.0 convert_reduce_fusion.10
  268.9 3.5 all-to-all-start.9
  272.4 7.4 %all-to-all-done.9 = bf16[2,16,2,1,256]{4,2,0,3,1:T(2,128)(2,1)S(1)} async-done(((bf16[2,16,2,1,256]{4,2,0,3,1:T(2,128)(2,1)}), bf16[2,16,2,1,256]{4,2,0,3,1:T(2,128)(2,1)S(1)}, u32[]{:S(2)}, u32[]{:S(2)}) %all-to-all-start.9) | async-done | bytes 32800 | tf_op jit(solution)/shard_map/all_to_all | solution.py:202
  280.7 3.5 all-to-all-start.10
  284.2 7.4 %all-to-all-done.10 = bf16[2,1,2,16,256]{4,2,0,1,3:T(2,128)(2,1)S(1)} async-done(((bf16[2,1,2,16,256]{4,2,0,1,3:T(2,128)(2,1)}), bf16[2,1,2,16,256]{4,2,0,1,3:T(2,128)(2,1)S(1)}, u32[]{:S(2)}, u32[]{:S(2)}) %all-to-all-start.10) | async-done | bytes 32800 | tf_op jit(solution)/shard_map/all_to_all | solution.py:191
  305.2 3.7 all-to-all-start.11
  308.9 2.2 convolution_add_fusion.19
  311.0 5.2 %all-to-all-done.11 = bf16[2,16,2,1,256]{4,2,0,3,1:T(2,128)(2,1)S(1)} async-done(((bf16[2,16,2,1,256]{4,2,0,3,1:T(2,128)(2,1)}), bf16[2,16,2,1,256]{4,2,0,3,1:T(2,128)(2,1)S(1)}, u32[]{:S(2)}, u32[]{:S(2)}) %all-to-all-start.11) | async-done | bytes 32800 | tf_op jit(solution)/shard_map/all_to_all | solution.py:202
  317.2 3.5 all-to-all-start.12
  320.8 7.3 %all-to-all-done.12 = bf16[2,1,2,16,256]{4,2,0,1,3:T(2,128)(2,1)S(1)} async-done(((bf16[2,1,2,16,256]{4,2,0,1,3:T(2,128)(2,1)}), bf16[2,1,2,16,256]{4,2,0,1,3:T(2,128)(2,1)S(1)}, u32[]{:S(2)}, u32[]{:S(2)}) %all-to-all-start.12) | async-done | bytes 32800 | tf_op jit(solution)/shard_map/all_to_all | solution.py:191
  339.6 38.5 %psum.79 = f32[2,1024]{1,0:T(2,128)S(1)} all-reduce(f32[2,1024]{1,0:T(2,128)S(1)} %fusion.164), channel_id=1, replica_groups=mesh['tm'=2,'lat'=16] {'tm','lat'}, use_global_device_ids=true, to_apply=%region_88.89 | all-reduce | flops 2048 | bytes 16384 | tf_op jit(solution)/shard_map/psum | solution.py:207
  378.8 90.0 %all-reduce.4.cloned.1.call-done = (f32[256,384]{1,0:T(8,128)}, f32[384,384]{1,0:T(8,128)}, f32[384,256]{1,0:T(8,128)}) async-done(((f32[256,384]{1,0:T(8,128)}, f32[384,384]{1,0:T(8,128)}, f32[384,256]{1,0:T(8,128)}), (f32[256,384]{1,0:T(8,128)}, f32[384,384]{1,0:T(8,128)}, f32[384,256]{1,0:T(8,128)})) %all-reduce.4.cloned.1.call-update) | async-done | bytes 1376272 | tf_op jit(solution)/shard_map/psum | solution.py:207
  (512 shorter events, 108.9 us)
Async XLA Ops:
  9.2 11.4 %copy-start.37 = (f32[256,384]{1,0:T(8,128)S(1)}, f32[256,384]{1,0:T(8,128)}, u32[]{:S(2)}) copy-start(f32[256,384]{1,0:T(8,128)} %param.26) | copy-start | bytes 1179652
  10.6 9.1 %copy-start.91 = (f32[2,1024]{1,0:T(2,128)S(1)}, f32[2,1024]{1,0:T(2,128)}, u32[]{:S(2)}) copy-start(f32[2,1024]{1,0:T(2,128)} %param.29) | copy-start | bytes 24580
  10.8 9.9 %copy-start.39 = (f32[384,256]{1,0:T(8,128)S(1)}, f32[384,256]{1,0:T(8,128)}, u32[]{:S(2)}) copy-start(f32[384,256]{1,0:T(8,128)} %param.28) | copy-start | bytes 1179652
  11.4 15.8 %all-to-all-start = ((bf16[2,1,2,16,256]{4,2,0,1,3:T(2,128)(2,1)}), bf16[2,1,2,16,256]{4,2,0,1,3:T(2,128)(2,1)S(1)}, u32[]{:S(2)}, u32[]{:S(2)}) async-start(bf16[2,1,2,16,256]{4,2,0,1,3:T(2,128)(2,1)} %copy.194), calls=%async_computation | async-start | bytes 65536 | tf_op jit(solution)/shard_map/all_to_all | solution.py:141
  19.8 73.5 %copy-start.139 = (f32[384]{0:T(512)}, f32[384]{0:T(512)S(1)}, u32[]{:S(2)}) copy-start(f32[384]{0:T(512)S(1)} %get-tuple-element.47) | copy-start | bytes 4612
  19.8 76.8 %copy-start.137 = (f32[384]{0:T(512)}, f32[384]{0:T(512)S(1)}, u32[]{:S(2)}) copy-start(f32[384]{0:T(512)S(1)} %get-tuple-element.45) | copy-start | bytes 4612
  20.6 72.7 %copy-start.24 = (bf16[256,384]{1,0:T(8,128)(2,1)}, bf16[256,384]{1,0:T(8,128)(2,1)S(1)}, u32[]{:S(2)}) copy-start(bf16[256,384]{1,0:T(8,128)(2,1)S(1)} %convert_element_type.413) | copy-start | bytes 589828
  21.8 74.9 %copy-start.21 = (bf16[384,384]{1,0:T(8,128)(2,1)}, bf16[384,384]{1,0:T(8,128)(2,1)S(1)}, u32[]{:S(2)}) copy-start(bf16[384,384]{1,0:T(8,128)(2,1)S(1)} %convert_element_type.415) | copy-start | bytes 884740
  28.0 3.0 copy-start.28
  31.0 4.0 copy-start.4
  31.9 3.2 copy-start.93
  60.6 3.0 copy-start.48
  63.7 4.0 copy-start.6
  64.5 3.2 copy-start.95
  93.4 3.1 copy-start.50
  96.5 3.4 copy-start.8
  96.6 3.2 copy-start.109
  96.6 3.2 copy-start.97
  113.0 3.9 copy-start.123
  113.0 19.9 %all-to-all-start.6 = ((bf16[2,1,2,16,256]{4,2,0,1,3:T(2,128)(2,1)}), bf16[2,1,2,16,256]{4,2,0,1,3:T(2,128)(2,1)S(1)}, u32[]{:S(2)}, u32[]{:S(2)}) async-start(bf16[2,1,2,16,256]{4,2,0,1,3:T(2,128)(2,1)} %copy.216), calls=%async_computation.6 | async-start | bytes 65536 | tf_op jit(solution)/shard_map/all_to_all | solution.py:141
  122.7 2.1 copy-start.11
  127.9 2.1 copy-start.13
  133.3 71.8 %copy-start.87 = (f32[1,2,2,128]{3,1,2,0:T(2,128)}, f32[1,2,2,128]{3,1,2,0:T(2,128)S(1)}, u32[]{:S(2)}) copy-start(f32[1,2,2,128]{3,1,2,0:T(2,128)S(1)} %copy.333) | copy-start | bytes 6148
  135.0 70.1 %copy-start.89 = (f32[512]{0:T(512)}, f32[512]{0:T(512)S(1)}, u32[]{:S(2)}) copy-start(f32[512]{0:T(512)S(1)} %rsqrt.155) | copy-start | bytes 6148
  136.3 3.1 copy-start.52
  139.4 4.4 copy-start.2
  139.5 4.2 copy-start.113
  140.6 3.2 copy-start.99
  208.6 5.5 %copy-start.136 = (f32[2,8]{1,0:T(2,128)S(1)}, f32[2,8]{1,0:T(2,128)}, u32[]{:S(2)}) copy-start(f32[2,8]{1,0:T(2,128)} %get-tuple-element.143) | copy-start | bytes 196
  230.8 3.7 copy-start.128
  230.8 11.0 %all-to-all-start.7 = ((bf16[2,16,2,1,256]{4,2,0,3,1:T(2,128)(2,1)}), bf16[2,16,2,1,256]{4,2,0,3,1:T(2,128)(2,1)S(1)}, u32[]{:S(2)}, u32[]{:S(2)}) async-start(bf16[2,16,2,1,256]{4,2,0,3,1:T(2,128)(2,1)} %copy.228), calls=%async_computation.7 | async-start | bytes 65536 | tf_op jit(solution)/shard_map/all_to_all | solution.py:202
  242.8 10.9 %all-to-all-start.8 = ((bf16[2,1,2,16,256]{4,2,0,1,3:T(2,128)(2,1)}), bf16[2,1,2,16,256]{4,2,0,1,3:T(2,128)(2,1)S(1)}, u32[]{:S(2)}, u32[]{:S(2)}) async-start(bf16[2,1,2,16,256]{4,2,0,1,3:T(2,128)(2,1)} %copy.231), calls=%async_computation.8 | async-start | bytes 65536 | tf_op jit(solution)/shard_map/all_to_all | solution.py:191
  265.1 2.2 copy-start.120
  268.0 23.6 %copy-start.36 = (f32[2,1,256,256]{3,2,0,1:T(8,128)S(1)}, f32[2,1,256,256]{3,2,0,1:T(8,128)}, u32[]{:S(2)}) copy-start(f32[2,1,256,256]{3,2,0,1:T(8,128)} %copy.243) | copy-start | bytes 1572868
  268.9 10.9 %all-to-all-start.9 = ((bf16[2,16,2,1,256]{4,2,0,3,1:T(2,128)(2,1)}), bf16[2,16,2,1,256]{4,2,0,3,1:T(2,128)(2,1)S(1)}, u32[]{:S(2)}, u32[]{:S(2)}) async-start(bf16[2,16,2,1,256]{4,2,0,3,1:T(2,128)(2,1)} %copy.238), calls=%async_computation.9 | async-start | bytes 65536 | tf_op jit(solution)/shard_map/all_to_all | solution.py:202
  280.7 10.9 %all-to-all-start.10 = ((bf16[2,1,2,16,256]{4,2,0,1,3:T(2,128)(2,1)}), bf16[2,1,2,16,256]{4,2,0,1,3:T(2,128)(2,1)S(1)}, u32[]{:S(2)}, u32[]{:S(2)}) async-start(bf16[2,1,2,16,256]{4,2,0,1,3:T(2,128)(2,1)} %copy.241), calls=%async_computation.10 | async-start | bytes 65536 | tf_op jit(solution)/shard_map/all_to_all | solution.py:191
  304.3 4.5 copy-start.49
  305.2 11.0 %all-to-all-start.11 = ((bf16[2,16,2,1,256]{4,2,0,3,1:T(2,128)(2,1)}), bf16[2,16,2,1,256]{4,2,0,3,1:T(2,128)(2,1)S(1)}, u32[]{:S(2)}, u32[]{:S(2)}) async-start(bf16[2,16,2,1,256]{4,2,0,3,1:T(2,128)(2,1)} %copy.248), calls=%async_computation.11 | async-start | bytes 65536 | tf_op jit(solution)/shard_map/all_to_all | solution.py:202
  308.9 19.2 %copy-start.35 = (f32[2,1,256,256]{3,2,0,1:T(8,128)S(1)}, f32[2,1,256,256]{3,2,0,1:T(8,128)}, u32[]{:S(2)}) copy-start(f32[2,1,256,256]{3,2,0,1:T(8,128)} %copy.253) | copy-start | bytes 1572868
  317.2 10.9 %all-to-all-start.12 = ((bf16[2,1,2,16,256]{4,2,0,1,3:T(2,128)(2,1)}), bf16[2,1,2,16,256]{4,2,0,1,3:T(2,128)(2,1)S(1)}, u32[]{:S(2)}, u32[]{:S(2)}) async-start(bf16[2,1,2,16,256]{4,2,0,1,3:T(2,128)(2,1)} %copy.251), calls=%async_computation.12 | async-start | bytes 65536 | tf_op jit(solution)/shard_map/all_to_all | solution.py:191
  320.7 148.0 %all-reduce.4.cloned.1.call-start = ((), (), s32[]{:S(2)}) async-start(), calls=%async_computation.13 | async-start | bytes 2752512 | tf_op jit(solution)/shard_map/psum | solution.py:207
  339.2 137.3 %copy-start.72 = (f32[256,384]{1,0:T(8,128)S(1)}, f32[256,384]{1,0:T(8,128)}, u32[]{:S(2)}) copy-start(f32[256,384]{1,0:T(8,128)} %param.30) | copy-start | bytes 1179652
  468.7 7.7 %copy-start.71 = (f32[256,384]{1,0:T(8,128)S(1)}, f32[256,384]{1,0:T(8,128)}, u32[]{:S(2)}) copy-start(f32[256,384]{1,0:T(8,128)} %param.34) | copy-start | bytes 1179652
  470.5 6.0 %copy-start.38 = (f32[256,384]{1,0:T(8,128)S(1)}, f32[256,384]{1,0:T(8,128)}, u32[]{:S(2)}) copy-start(f32[256,384]{1,0:T(8,128)} %param.26) | copy-start | bytes 1179652
  472.4 3.4 copy-start.129
  472.4 3.4 copy-start.130
  473.1 2.7 copy-start.92
  478.3 2.1 copy-start.70
  (104 other events, 121.1 us)
Sparse Core Ops, SparseCore 0:
  339.3 129.3 all-reduce.3
where the time goes:
time: 499 us; the launch traced here: 491 us
  waiting for transfers between devices  136 us (27%)
  blocking collectives  134 us (27%)
  matrix products  61.3 us (12%)
  local copies, waits for them, and re-layouts  61.2 us (12%)
  other arithmetic  44.3 us (9%)
  starting transfers between devices  33.5 us (7%)
  between operations  20.2 us (4%)
    psum x1, waiting for transfers between devices, per_device(): grads = lax.psum(totals, ('tm', 'lat'))  90 us
    psum x1, blocking collectives, per_device(): num_total, den_total = lax.psum((num_part, den_part), 'lat')  42.5 us
    psum x1, blocking collectives, per_device(): grads = lax.psum(totals, ('tm', 'lat'))  38.5 us
    dot_general x12, matrix products, corrector_forward(): jnp.dot(h_low, weights[k], preferred_element_type=jnp.float32)  31.7 us
    all_to_all x3, blocking collectives, per_device(): lax.all_to_all(coeff, 'lat', split_axis=1, concat_axis=3, tiled=True)  29.9 us
    unnamed x297, local copies, waits for them, and re-layouts  29.6 us
    all_to_all x3, waiting for transfers between devices, per_device(): lax.all_to_all(back_coeff, 'lat', split_axis=3, concat_axis=1, tiled=True)  21.3 us
    all_to_all x2, blocking collectives, to_grid(): lax.all_to_all(sums, 'lat', split_axis=3, concat_axis=1, tiled=True)  20.1 us
  transfers between devices with their start and end apart: 9, of which 8 were waited for; matrix products, arithmetic and copies ran while one was open for 4% of the time, Pallas kernels for 0%

commit v1 on v0

--- a/solution.py
+++ b/solution.py
@@ -15,6 +15,22 @@
 EPS_ADAM = 1e-08
 DECAY = 0.1
 HIGH = lax.Precision.HIGHEST
+
+
+def exchange_in_pairs(shard, axis, split, join):
+    ways, here = (lax.axis_size(axis), lax.axis_index(axis))
+    width = shard.shape[split] // ways
+    shape = list(shard.shape)
+    shape[split] = width
+    height = shape[join]
+    shape[join] = height * ways
+    full = jnp.zeros(shape, shard.dtype)
+    for mask in range(ways):
+        part = lax.dynamic_slice_in_dim(shard, (here ^ mask) * width, width, axis=split)
+        if mask:
+            part = lax.ppermute(part, axis, [(d, d ^ mask) for d in range(ways)])
+        full = lax.dynamic_update_slice_in_dim(full, part, (here ^ mask) * height, axis=join)
+    return full
 
 
 def wave_tables(wave_slots, lon_count):
@@ -187,9 +203,7 @@
             back_coeff = jnp.einsum(
                 "mnr,tmpnc->tmprc", plg, back_spec, preferred_element_type=jnp.float32
             ).astype(jnp.bfloat16)
-            back_tend = fourier_sum(
-                ffw, lax.all_to_all(back_coeff, "lat", split_axis=3, concat_axis=1, tiled=True)
-            )
+            back_tend = fourier_sum(ffw, exchange_in_pairs(back_coeff, "lat", 3, 1))
             back_out = back_out + qlocal[None, :, None, None] * back_tend
         back_in, grads = corrector_backward(back_out.reshape(-1, chans), saved, weights, norm_bias)
         totals = tuple((a + b for a, b in zip(totals, grads)))

time: 499 us -> 575 us (1.15)
  starting transfers between devices: 33.5 us -> 106 us
  waiting for transfers between devices: 136 us -> 117 us
  local copies, waits for them, and re-layouts: 61.2 us -> 71.2 us
  other arithmetic: 44.3 us -> 51.9 us
    ppermute x0 -> x45, starting transfers between devices: none -> 79.9 us  [exchange_in_pairs(): part = lax.ppermute(part, axis, [(d, d ^ mask) for d in range(ways)])]
    all_to_all x3 -> x0, waiting for transfers between devices: 21.3 us -> none  [per_device(): lax.all_to_all(back_coeff, 'lat', split_axis=3, concat_axis=1, tiled=True)]
    all_to_all x3 -> x0, starting transfers between devices: 10.5 us -> none  [per_device(): lax.all_to_all(back_coeff, 'lat', split_axis=3, concat_axis=1, tiled=True)]
    another operation x0 -> x51, local copies, waits for them, and re-layouts: none -> 7.91 us
    unnamed x297 -> x385, local copies, waits for them, and re-layouts: 29.6 us -> 35.6 us
  transfers between devices with their start and end apart: 9 -> 51, of which waited for: 8 -> 8; matrix products, arithmetic and copies ran while one was open for 4% -> 8% of each run, Pallas kernels for 0% -> 0%
where the time goes in v1:
time: 575 us; the launch traced here: 566 us
  blocking collectives  135 us (23%)
  waiting for transfers between devices  117 us (20%)
  starting transfers between devices  106 us (18%)
  local copies, waits for them, and re-layouts  71.2 us (12%)
  matrix products  64.6 us (11%)
  other arithmetic  51.9 us (9%)
  between operations  20.9 us (4%)
    psum x1, waiting for transfers between devices, per_device(): grads = lax.psum(totals, ('tm', 'lat'))  92.1 us
    ppermute x45, starting transfers between devices, exchange_in_pairs(): part = lax.ppermute(part, axis, [(d, d ^ mask) for d in range(ways)])  79.9 us
    psum x1, blocking collectives, per_device(): num_total, den_total = lax.psum((num_part, den_part), 'lat')  42.6 us
    psum x1, blocking collectives, per_device(): grads = lax.psum(totals, ('tm', 'lat'))  39.6 us
    unnamed x385, local copies, waits for them, and re-layouts  35.6 us
    dot_general x12, matrix products, corrector_forward(): jnp.dot(h_low, weights[k], preferred_element_type=jnp.float32)  31.7 us
    all_to_all x3, blocking collectives, per_device(): lax.all_to_all(coeff, 'lat', split_axis=1, concat_axis=3, tiled=True)  29.9 us
    all_to_all x2, blocking collectives, to_grid(): lax.all_to_all(sums, 'lat', split_axis=3, concat_axis=1, tiled=True)  20.1 us
  transfers between devices with their start and end apart: 51, of which 8 were waited for; matrix products, arithmetic and copies ran while one was open for 8% of the time, Pallas kernels for 0%

profile of v1, /device:TPU:0, one launch (start us, length us, event | category | flops | bytes accessed | tf_op | source)
XLA Modules:
  0.0 566.5 jit_solution(8622951941645543158)
XLA Ops:
  11.4 8.3 %all-to-all-start = ((bf16[2,1,2,16,256]{4,2,0,1,3:T(2,128)(2,1)}), bf16[2,1,2,16,256]{4,2,0,1,3:T(2,128)(2,1)S(1)}, u32[]{:S(2)}, u32[]{:S(2)}) async-start(bf16[2,1,2,16,256]{4,2,0,1,3:T(2,128)(2,1)} %copy.278), calls=%async_computation | async-start | bytes 65536 | tf_op jit(solution)/shard_map/all_to_all | solution.py:157
  21.8 5.3 all-to-all-done
  28.0 3.0 fusion.208
  31.9 3.2 fusion.206
  37.8 10.0 %all_to_all.170 = bf16[2,16,2,1,256]{4,2,0,3,1:T(2,128)(2,1)S(1)} all-to-all(bf16[2,16,2,1,256]{4,2,0,3,1:T(2,128)(2,1)S(1)} %copy.282), channel_id=1, replica_groups=mesh['tm'=2,'lat'=16] {'lat'}, dimensions={1} | all-to-all | bytes 65536 | tf_op jit(solution)/shard_map/all_to_all | solution.py:185
  48.1 10.1 %all_to_all.171 = bf16[2,1,2,16,256]{4,2,0,1,3:T(2,128)(2,1)S(1)} all-to-all(bf16[2,1,2,16,256]{4,2,0,1,3:T(2,128)(2,1)S(1)} %copy.286), channel_id=1, replica_groups=mesh['tm'=2,'lat'=16] {'lat'}, dimensions={3} | all-to-all | bytes 65536 | tf_op jit(solution)/shard_map/all_to_all | solution.py:157
  60.6 3.0 fusion.204
  64.5 3.2 fusion.202
  70.5 10.0 %all_to_all.172 = bf16[2,16,2,1,256]{4,2,0,3,1:T(2,128)(2,1)S(1)} all-to-all(bf16[2,16,2,1,256]{4,2,0,3,1:T(2,128)(2,1)S(1)} %copy.290), channel_id=1, replica_groups=mesh['tm'=2,'lat'=16] {'lat'}, dimensions={1} | all-to-all | bytes 65536 | tf_op jit(solution)/shard_map/all_to_all | solution.py:185
  80.8 10.0 %all_to_all.173 = bf16[2,1,2,16,256]{4,2,0,1,3:T(2,128)(2,1)S(1)} all-to-all(bf16[2,1,2,16,256]{4,2,0,1,3:T(2,128)(2,1)S(1)} %copy.293), channel_id=1, replica_groups=mesh['tm'=2,'lat'=16] {'lat'}, dimensions={3} | all-to-all | bytes 65536 | tf_op jit(solution)/shard_map/all_to_all | solution.py:157
  93.4 3.1 fusion.200
  96.6 3.2 fusion.198
  102.0 10.0 %all_to_all.174 = bf16[2,16,2,1,256]{4,2,0,3,1:T(2,128)(2,1)S(1)} all-to-all(bf16[2,16,2,1,256]{4,2,0,3,1:T(2,128)(2,1)S(1)} %copy.297), channel_id=1, replica_groups=mesh['tm'=2,'lat'=16] {'lat'}, dimensions={1} | all-to-all | bytes 65536 | tf_op jit(solution)/shard_map/all_to_all | solution.py:185
  113.0 3.8 all-to-all-start.6
  123.3 2.1 copy.289
  136.8 3.1 fusion.196
  141.1 3.2 fusion.194
  151.6 42.6 %all-reduce.1 = (f32[1,2,8]{2,1,0:T(2,128)S(1)}, f32[1,2,8]{2,1,0:T(2,128)S(1)}, f32[1,2,8]{2,1,0:T(2,128)S(1)}, f32[1,2,8]{2,1,0:T(2,128)S(1)}, f32[2,8]{1,0:T(2,128)S(1)}) all-reduce(f32[1,2,8]{2,1,0:T(2,128)S(1)} %bitcast.827, f32[1,2,8]{2,1,0:T(2,128)S(1)} %bitcast.828, ...), channel_id=1, replica_groups=mesh['tm'=2,'lat'=16] {'lat'}, use_global_device_ids=true, to_apply=%region_31.32 | all-reduce | flops 80 | bytes 640 | tf_op jit(solution)/shard_map/psum | solution.py:179
  214.6 4.0 all-to-all-start.7
  219.2 6.3 %all-to-all-done.7 = bf16[2,16,2,1,256]{4,2,0,3,1:T(2,128)(2,1)S(1)} async-done(((bf16[2,16,2,1,256]{4,2,0,3,1:T(2,128)(2,1)}), bf16[2,16,2,1,256]{4,2,0,3,1:T(2,128)(2,1)S(1)}, u32[]{:S(2)}, u32[]{:S(2)}) %all-to-all-start.7) | async-done | bytes 32800 | tf_op jit(solution)/shard_map/all_to_all | solution.py:216
  227.7 2.3 collective-permute-start.2
  237.6 3.2 collective-permute-start.6
  241.5 2.5 collective-permute-start.8
  245.9 3.0 psum.75
  254.5 4.0 collective-permute-start.10
  259.2 3.3 collective-permute-start.12
  263.1 4.9 collective-permute-start.14
  278.3 2.5 convert_reduce_fusion.10
  295.5 3.5 all-to-all-start.8
  301.1 5.3 all-to-all-done.8
  308.1 2.3 collective-permute-start.17
  312.6 2.2 convolution_add_fusion.20
  315.4 3.2 collective-permute-start.21
  319.3 2.4 collective-permute-start.23
  323.0 4.1 collective-permute-start.25
  327.8 3.3 collective-permute-start.27
  331.6 4.9 collective-permute-start.29
  353.7 6.3 %all-to-all-start.9 = ((bf16[2,16,2,1,256]{4,2,0,3,1:T(2,128)(2,1)}), bf16[2,16,2,1,256]{4,2,0,3,1:T(2,128)(2,1)S(1)}, u32[]{:S(2)}, u32[]{:S(2)}) async-start(bf16[2,16,2,1,256]{4,2,0,3,1:T(2,128)(2,1)} %copy.358), calls=%async_computation.9 | async-start | bytes 65536 | tf_op jit(solution)/shard_map/all_to_all | solution.py:216
  360.1 2.4 convolution_add_fusion.9
  362.5 4.9 all-to-all-done.9
  369.1 2.3 collective-permute-start.32
  375.6 3.2 collective-permute-start.36
  379.4 2.4 collective-permute-start.38
  383.6 4.1 collective-permute-start.40
  388.4 3.2 collective-permute-start.42
  392.3 4.9 collective-permute-start.44
  412.1 39.6 %psum.79 = f32[2,1024]{1,0:T(2,128)S(1)} all-reduce(f32[2,1024]{1,0:T(2,128)S(1)} %fusion.155), channel_id=1, replica_groups=mesh['tm'=2,'lat'=16] {'tm','lat'}, use_global_device_ids=true, to_apply=%region_88.89 | all-reduce | flops 2048 | bytes 16384 | tf_op jit(solution)/shard_map/psum | solution.py:221
  452.4 92.1 %all-reduce.4.cloned.1.call-done = (f32[256,384]{1,0:T(8,128)}, f32[384,384]{1,0:T(8,128)}, f32[384,256]{1,0:T(8,128)}) async-done(((f32[256,384]{1,0:T(8,128)}, f32[384,384]{1,0:T(8,128)}, f32[384,256]{1,0:T(8,128)}), (f32[256,384]{1,0:T(8,128)}, f32[384,384]{1,0:T(8,128)}, f32[384,256]{1,0:T(8,128)})) %all-reduce.4.cloned.1.call-update) | async-done | bytes 1376272 | tf_op jit(solution)/shard_map/psum | solution.py:221
  (779 shorter events, 175.9 us)
Async XLA Ops:
  11.4 15.8 %all-to-all-start = ((bf16[2,1,2,16,256]{4,2,0,1,3:T(2,128)(2,1)}), bf16[2,1,2,16,256]{4,2,0,1,3:T(2,128)(2,1)S(1)}, u32[]{:S(2)}, u32[]{:S(2)}) async-start(bf16[2,1,2,16,256]{4,2,0,1,3:T(2,128)(2,1)} %copy.278), calls=%async_computation | async-start | bytes 65536 | tf_op jit(solution)/shard_map/all_to_all | solution.py:157
  113.0 20.5 %all-to-all-start.6 = ((bf16[2,1,2,16,256]{4,2,0,1,3:T(2,128)(2,1)}), bf16[2,1,2,16,256]{4,2,0,1,3:T(2,128)(2,1)S(1)}, u32[]{:S(2)}, u32[]{:S(2)}) async-start(bf16[2,1,2,16,256]{4,2,0,1,3:T(2,128)(2,1)} %copy.300), calls=%async_computation.6 | async-start | bytes 65536 | tf_op jit(solution)/shard_map/all_to_all | solution.py:157
  214.6 10.9 %all-to-all-start.7 = ((bf16[2,16,2,1,256]{4,2,0,3,1:T(2,128)(2,1)}), bf16[2,16,2,1,256]{4,2,0,3,1:T(2,128)(2,1)S(1)}, u32[]{:S(2)}, u32[]{:S(2)}) async-start(bf16[2,16,2,1,256]{4,2,0,3,1:T(2,128)(2,1)} %copy.312), calls=%async_computation.7 | async-start | bytes 65536 | tf_op jit(solution)/shard_map/all_to_all | solution.py:216
  226.5 10.6 %collective-permute-start = (bf16[2,1,2,1,256]{4,2,0,3,1:T(2,128)(2,1)S(1)}, bf16[2,1,2,1,256]{4,2,0,3,1:T(2,128)(2,1)S(1)}, u32[]{:S(2)}, u32[]{:S(2)}) collective-permute-start(bf16[2,1,2,1,256]{4,2,0,3,1:T(2,128)(2,1)S(1)} %bitcast.897), channel_id=1, source_target_pairs={{0,1},{1,0},{2,3},{3,2},{4,5},{5,4},{6,7},{7,6},{8,9},{9,8},{10,11... | collective-permute-start | bytes 6152 | tf_op jit(solution)/shard_map/ppermute | solution.py:31
  227.3 10.3 %collective-permute-start.1 = (bf16[2,1,2,1,256]{4,2,0,3,1:T(2,128)(2,1)S(1)}, bf16[2,1,2,1,256]{4,2,0,3,1:T(2,128)(2,1)S(1)}, u32[]{:S(2)}, u32[]{:S(2)}) collective-permute-start(bf16[2,1,2,1,256]{4,2,0,3,1:T(2,128)(2,1)S(1)} %bitcast.894), channel_id=1, source_target_pairs={{0,2},{1,3},{2,0},{3,1},{4,6},{5,7},{6,4},{7,5},{8,10},{9,11},{10,... | collective-permute-start | bytes 6152 | tf_op jit(solution)/shard_map/ppermute | solution.py:31
  227.7 13.1 %collective-permute-start.2 = (bf16[2,1,2,1,256]{4,2,0,3,1:T(2,128)(2,1)S(1)}, bf16[2,1,2,1,256]{4,2,0,3,1:T(2,128)(2,1)S(1)}, u32[]{:S(2)}, u32[]{:S(2)}) collective-permute-start(bf16[2,1,2,1,256]{4,2,0,3,1:T(2,128)(2,1)S(1)} %bitcast.889), channel_id=1, source_target_pairs={{0,3},{1,2},{2,1},{3,0},{4,7},{5,6},{6,5},{7,4},{8,11},{9,10},{10,... | collective-permute-start | bytes 6152 | tf_op jit(solution)/shard_map/ppermute | solution.py:31
  230.1 11.4 %collective-permute-start.3 = (bf16[2,1,2,1,256]{4,2,0,3,1:T(2,128)(2,1)S(1)}, bf16[2,1,2,1,256]{4,2,0,3,1:T(2,128)(2,1)S(1)}, u32[]{:S(2)}, u32[]{:S(2)}) collective-permute-start(bf16[2,1,2,1,256]{4,2,0,3,1:T(2,128)(2,1)S(1)} %bitcast.875), channel_id=1, source_target_pairs={{0,4},{1,5},{2,6},{3,7},{4,0},{5,1},{6,2},{7,3},{8,12},{9,13},{10,... | collective-permute-start | bytes 6152 | tf_op jit(solution)/shard_map/ppermute | solution.py:31
  230.7 13.3 %collective-permute-start.4 = (bf16[2,1,2,1,256]{4,2,0,3,1:T(2,128)(2,1)S(1)}, bf16[2,1,2,1,256]{4,2,0,3,1:T(2,128)(2,1)S(1)}, u32[]{:S(2)}, u32[]{:S(2)}) collective-permute-start(bf16[2,1,2,1,256]{4,2,0,3,1:T(2,128)(2,1)S(1)} %bitcast.867), channel_id=1, source_target_pairs={{0,5},{1,4},{2,7},{3,6},{4,1},{5,0},{6,3},{7,2},{8,13},{9,12},{10,... | collective-permute-start | bytes 6152 | tf_op jit(solution)/shard_map/ppermute | solution.py:31
  237.1 17.4 %collective-permute-start.5 = (bf16[2,1,2,1,256]{4,2,0,3,1:T(2,128)(2,1)}, bf16[2,1,2,1,256]{4,2,0,3,1:T(2,128)(2,1)}, u32[]{:S(2)}, u32[]{:S(2)}) collective-permute-start(bf16[2,1,2,1,256]{4,2,0,3,1:T(2,128)(2,1)} %bitcast.751), channel_id=1, source_target_pairs={{0,6},{1,7},{2,4},{3,5},{4,2},{5,3},{6,0},{7,1},{8,14},{9,15},{10,... | collective-permute-start | bytes 6152 | tf_op jit(solution)/shard_map/ppermute | solution.py:31
  237.6 20.9 %collective-permute-start.6 = (bf16[2,1,2,1,256]{4,2,0,3,1:T(2,128)(2,1)}, bf16[2,1,2,1,256]{4,2,0,3,1:T(2,128)(2,1)}, u32[]{:S(2)}, u32[]{:S(2)}) collective-permute-start(bf16[2,1,2,1,256]{4,2,0,3,1:T(2,128)(2,1)} %bitcast.750), channel_id=1, source_target_pairs={{0,7},{1,6},{2,5},{3,4},{4,3},{5,2},{6,1},{7,0},{8,15},{9,14},{10,... | collective-permute-start | bytes 6152 | tf_op jit(solution)/shard_map/ppermute | solution.py:31
  240.8 18.4 %collective-permute-start.7 = (bf16[2,1,2,1,256]{4,2,0,3,1:T(2,128)(2,1)}, bf16[2,1,2,1,256]{4,2,0,3,1:T(2,128)(2,1)}, u32[]{:S(2)}, u32[]{:S(2)}) collective-permute-start(bf16[2,1,2,1,256]{4,2,0,3,1:T(2,128)(2,1)} %bitcast.749), channel_id=1, source_target_pairs={{0,8},{1,9},{2,10},{3,11},{4,12},{5,13},{6,14},{7,15},{8,0},{9,1},... | collective-permute-start | bytes 6152 | tf_op jit(solution)/shard_map/ppermute | solution.py:31
  241.5 21.0 %collective-permute-start.8 = (bf16[2,1,2,1,256]{4,2,0,3,1:T(2,128)(2,1)}, bf16[2,1,2,1,256]{4,2,0,3,1:T(2,128)(2,1)}, u32[]{:S(2)}, u32[]{:S(2)}) collective-permute-start(bf16[2,1,2,1,256]{4,2,0,3,1:T(2,128)(2,1)} %bitcast.748), channel_id=1, source_target_pairs={{0,9},{1,8},{2,11},{3,10},{4,13},{5,12},{6,15},{7,14},{8,1},{9,0},... | collective-permute-start | bytes 6152 | tf_op jit(solution)/shard_map/ppermute | solution.py:31
  244.0 19.1 %collective-permute-start.9 = (bf16[2,1,2,1,256]{4,2,0,3,1:T(2,128)(2,1)}, bf16[2,1,2,1,256]{4,2,0,3,1:T(2,128)(2,1)}, u32[]{:S(2)}, u32[]{:S(2)}) collective-permute-start(bf16[2,1,2,1,256]{4,2,0,3,1:T(2,128)(2,1)} %bitcast.747), channel_id=1, source_target_pairs={{0,10},{1,11},{2,8},{3,9},{4,14},{5,15},{6,12},{7,13},{8,2},{9,3},... | collective-permute-start | bytes 6152 | tf_op jit(solution)/shard_map/ppermute | solution.py:31
  254.5 19.7 %collective-permute-start.10 = (bf16[2,1,2,1,256]{4,2,0,3,1:T(2,128)(2,1)}, bf16[2,1,2,1,256]{4,2,0,3,1:T(2,128)(2,1)}, u32[]{:S(2)}, u32[]{:S(2)}) collective-permute-start(bf16[2,1,2,1,256]{4,2,0,3,1:T(2,128)(2,1)} %bitcast.746), channel_id=1, source_target_pairs={{0,11},{1,10},{2,9},{3,8},{4,15},{5,14},{6,13},{7,12},{8,3},{9,2},... | collective-permute-start | bytes 6152 | tf_op jit(solution)/shard_map/ppermute | solution.py:31
  258.5 16.4 %collective-permute-start.11 = (bf16[2,1,2,1,256]{4,2,0,3,1:T(2,128)(2,1)}, bf16[2,1,2,1,256]{4,2,0,3,1:T(2,128)(2,1)}, u32[]{:S(2)}, u32[]{:S(2)}) collective-permute-start(bf16[2,1,2,1,256]{4,2,0,3,1:T(2,128)(2,1)} %bitcast.745), channel_id=1, source_target_pairs={{0,12},{1,13},{2,14},{3,15},{4,8},{5,9},{6,10},{7,11},{8,4},{9,5},... | collective-permute-start | bytes 6152 | tf_op jit(solution)/shard_map/ppermute | solution.py:31
  259.2 16.4 %collective-permute-start.12 = (bf16[2,1,2,1,256]{4,2,0,3,1:T(2,128)(2,1)}, bf16[2,1,2,1,256]{4,2,0,3,1:T(2,128)(2,1)}, u32[]{:S(2)}, u32[]{:S(2)}) collective-permute-start(bf16[2,1,2,1,256]{4,2,0,3,1:T(2,128)(2,1)} %bitcast.744), channel_id=1, source_target_pairs={{0,13},{1,12},{2,15},{3,14},{4,9},{5,8},{6,11},{7,10},{8,5},{9,4},... | collective-permute-start | bytes 6152 | tf_op jit(solution)/shard_map/ppermute | solution.py:31
  262.5 13.8 %collective-permute-start.13 = (bf16[2,1,2,1,256]{4,2,0,3,1:T(2,128)(2,1)}, bf16[2,1,2,1,256]{4,2,0,3,1:T(2,128)(2,1)}, u32[]{:S(2)}, u32[]{:S(2)}) collective-permute-start(bf16[2,1,2,1,256]{4,2,0,3,1:T(2,128)(2,1)} %bitcast.743), channel_id=1, source_target_pairs={{0,14},{1,15},{2,12},{3,13},{4,10},{5,11},{6,8},{7,9},{8,6},{9,7},... | collective-permute-start | bytes 6152 | tf_op jit(solution)/shard_map/ppermute | solution.py:31
  263.1 13.9 %collective-permute-start.14 = (bf16[2,1,2,1,256]{4,2,0,3,1:T(2,128)(2,1)}, bf16[2,1,2,1,256]{4,2,0,3,1:T(2,128)(2,1)}, u32[]{:S(2)}, u32[]{:S(2)}) collective-permute-start(bf16[2,1,2,1,256]{4,2,0,3,1:T(2,128)(2,1)} %bitcast.742), channel_id=1, source_target_pairs={{0,15},{1,14},{2,13},{3,12},{4,11},{5,10},{6,9},{7,8},{8,7},{9,6},... | collective-permute-start | bytes 6152 | tf_op jit(solution)/shard_map/ppermute | solution.py:31
  295.5 10.9 %all-to-all-start.8 = ((bf16[2,16,2,1,256]{4,2,0,3,1:T(2,128)(2,1)}), bf16[2,16,2,1,256]{4,2,0,3,1:T(2,128)(2,1)S(1)}, u32[]{:S(2)}, u32[]{:S(2)}) async-start(bf16[2,16,2,1,256]{4,2,0,3,1:T(2,128)(2,1)} %copy.335), calls=%async_computation.8 | async-start | bytes 65536 | tf_op jit(solution)/shard_map/all_to_all | solution.py:216
  306.9 7.9 %collective-permute-start.15 = (bf16[2,1,2,1,256]{4,2,0,3,1:T(2,128)(2,1)S(1)}, bf16[2,1,2,1,256]{4,2,0,3,1:T(2,128)(2,1)S(1)}, u32[]{:S(2)}, u32[]{:S(2)}) collective-permute-start(bf16[2,1,2,1,256]{4,2,0,3,1:T(2,128)(2,1)S(1)} %bitcast.899), channel_id=1, source_target_pairs={{0,1},{1,0},{2,3},{3,2},{4,5},{5,4},{6,7},{7,6},{8,9},{9,8},{10,11... | collective-permute-start | bytes 6152 | tf_op jit(solution)/shard_map/ppermute | solution.py:31
  307.7 7.8 %collective-permute-start.16 = (bf16[2,1,2,1,256]{4,2,0,3,1:T(2,128)(2,1)S(1)}, bf16[2,1,2,1,256]{4,2,0,3,1:T(2,128)(2,1)S(1)}, u32[]{:S(2)}, u32[]{:S(2)}) collective-permute-start(bf16[2,1,2,1,256]{4,2,0,3,1:T(2,128)(2,1)S(1)} %bitcast.896), channel_id=1, source_target_pairs={{0,2},{1,3},{2,0},{3,1},{4,6},{5,7},{6,4},{7,5},{8,10},{9,11},{10,... | collective-permute-start | bytes 6152 | tf_op jit(solution)/shard_map/ppermute | solution.py:31
  308.1 10.5 %collective-permute-start.17 = (bf16[2,1,2,1,256]{4,2,0,3,1:T(2,128)(2,1)S(1)}, bf16[2,1,2,1,256]{4,2,0,3,1:T(2,128)(2,1)S(1)}, u32[]{:S(2)}, u32[]{:S(2)}) collective-permute-start(bf16[2,1,2,1,256]{4,2,0,3,1:T(2,128)(2,1)S(1)} %bitcast.892), channel_id=1, source_target_pairs={{0,3},{1,2},{2,1},{3,0},{4,7},{5,6},{6,5},{7,4},{8,11},{9,10},{10,... | collective-permute-start | bytes 6152 | tf_op jit(solution)/shard_map/ppermute | solution.py:31
  310.4 8.8 %collective-permute-start.18 = (bf16[2,1,2,1,256]{4,2,0,3,1:T(2,128)(2,1)S(1)}, bf16[2,1,2,1,256]{4,2,0,3,1:T(2,128)(2,1)S(1)}, u32[]{:S(2)}, u32[]{:S(2)}) collective-permute-start(bf16[2,1,2,1,256]{4,2,0,3,1:T(2,128)(2,1)S(1)} %bitcast.882), channel_id=1, source_target_pairs={{0,4},{1,5},{2,6},{3,7},{4,0},{5,1},{6,2},{7,3},{8,12},{9,13},{10,... | collective-permute-start | bytes 6152 | tf_op jit(solution)/shard_map/ppermute | solution.py:31
  311.1 10.6 %collective-permute-start.19 = (bf16[2,1,2,1,256]{4,2,0,3,1:T(2,128)(2,1)S(1)}, bf16[2,1,2,1,256]{4,2,0,3,1:T(2,128)(2,1)S(1)}, u32[]{:S(2)}, u32[]{:S(2)}) collective-permute-start(bf16[2,1,2,1,256]{4,2,0,3,1:T(2,128)(2,1)S(1)} %bitcast.870), channel_id=1, source_target_pairs={{0,5},{1,4},{2,7},{3,6},{4,1},{5,0},{6,3},{7,2},{8,13},{9,12},{10,... | collective-permute-start | bytes 6152 | tf_op jit(solution)/shard_map/ppermute | solution.py:31
  314.8 8.2 %collective-permute-start.20 = (bf16[2,1,2,1,256]{4,2,0,3,1:T(2,128)(2,1)S(1)}, bf16[2,1,2,1,256]{4,2,0,3,1:T(2,128)(2,1)S(1)}, u32[]{:S(2)}, u32[]{:S(2)}) collective-permute-start(bf16[2,1,2,1,256]{4,2,0,3,1:T(2,128)(2,1)S(1)} %bitcast.890), channel_id=1, source_target_pairs={{0,6},{1,7},{2,4},{3,5},{4,2},{5,3},{6,0},{7,1},{8,14},{9,15},{10,... | collective-permute-start | bytes 6152 | tf_op jit(solution)/shard_map/ppermute | solution.py:31
  315.4 11.7 %collective-permute-start.21 = (bf16[2,1,2,1,256]{4,2,0,3,1:T(2,128)(2,1)S(1)}, bf16[2,1,2,1,256]{4,2,0,3,1:T(2,128)(2,1)S(1)}, u32[]{:S(2)}, u32[]{:S(2)}) collective-permute-start(bf16[2,1,2,1,256]{4,2,0,3,1:T(2,128)(2,1)S(1)} %bitcast.878), channel_id=1, source_target_pairs={{0,7},{1,6},{2,5},{3,4},{4,3},{5,2},{6,1},{7,0},{8,15},{9,14},{10,... | collective-permute-start | bytes 6152 | tf_op jit(solution)/shard_map/ppermute | solution.py:31
  318.6 9.2 %collective-permute-start.22 = (bf16[2,1,2,1,256]{4,2,0,3,1:T(2,128)(2,1)S(1)}, bf16[2,1,2,1,256]{4,2,0,3,1:T(2,128)(2,1)S(1)}, u32[]{:S(2)}, u32[]{:S(2)}) collective-permute-start(bf16[2,1,2,1,256]{4,2,0,3,1:T(2,128)(2,1)S(1)} %bitcast.868), channel_id=1, source_target_pairs={{0,8},{1,9},{2,10},{3,11},{4,12},{5,13},{6,14},{7,15},{8,0},{9,1},... | collective-permute-start | bytes 6152 | tf_op jit(solution)/shard_map/ppermute | solution.py:31
  319.3 11.8 %collective-permute-start.23 = (bf16[2,1,2,1,256]{4,2,0,3,1:T(2,128)(2,1)S(1)}, bf16[2,1,2,1,256]{4,2,0,3,1:T(2,128)(2,1)S(1)}, u32[]{:S(2)}, u32[]{:S(2)}) collective-permute-start(bf16[2,1,2,1,256]{4,2,0,3,1:T(2,128)(2,1)S(1)} %bitcast.861), channel_id=1, source_target_pairs={{0,9},{1,8},{2,11},{3,10},{4,13},{5,12},{6,15},{7,14},{8,1},{9,0},... | collective-permute-start | bytes 6152 | tf_op jit(solution)/shard_map/ppermute | solution.py:31
  321.7 10.0 %collective-permute-start.24 = (bf16[2,1,2,1,256]{4,2,0,3,1:T(2,128)(2,1)S(1)}, bf16[2,1,2,1,256]{4,2,0,3,1:T(2,128)(2,1)S(1)}, u32[]{:S(2)}, u32[]{:S(2)}) collective-permute-start(bf16[2,1,2,1,256]{4,2,0,3,1:T(2,128)(2,1)S(1)} %bitcast.854), channel_id=1, source_target_pairs={{0,10},{1,11},{2,8},{3,9},{4,14},{5,15},{6,12},{7,13},{8,2},{9,3},... | collective-permute-start | bytes 6152 | tf_op jit(solution)/shard_map/ppermute | solution.py:31
  323.0 15.1 %collective-permute-start.25 = (bf16[2,1,2,1,256]{4,2,0,3,1:T(2,128)(2,1)S(1)}, bf16[2,1,2,1,256]{4,2,0,3,1:T(2,128)(2,1)S(1)}, u32[]{:S(2)}, u32[]{:S(2)}) collective-permute-start(bf16[2,1,2,1,256]{4,2,0,3,1:T(2,128)(2,1)S(1)} %bitcast.873), channel_id=1, source_target_pairs={{0,11},{1,10},{2,9},{3,8},{4,15},{5,14},{6,13},{7,12},{8,3},{9,2},... | collective-permute-start | bytes 6152 | tf_op jit(solution)/shard_map/ppermute | solution.py:31
  327.1 11.0 %collective-permute-start.26 = (bf16[2,1,2,1,256]{4,2,0,3,1:T(2,128)(2,1)S(1)}, bf16[2,1,2,1,256]{4,2,0,3,1:T(2,128)(2,1)S(1)}, u32[]{:S(2)}, u32[]{:S(2)}) collective-permute-start(bf16[2,1,2,1,256]{4,2,0,3,1:T(2,128)(2,1)S(1)} %bitcast.866), channel_id=1, source_target_pairs={{0,12},{1,13},{2,14},{3,15},{4,8},{5,9},{6,10},{7,11},{8,4},{9,5},... | collective-permute-start | bytes 6152 | tf_op jit(solution)/shard_map/ppermute | solution.py:31
  327.8 10.3 %collective-permute-start.27 = (bf16[2,1,2,1,256]{4,2,0,3,1:T(2,128)(2,1)S(1)}, bf16[2,1,2,1,256]{4,2,0,3,1:T(2,128)(2,1)S(1)}, u32[]{:S(2)}, u32[]{:S(2)}) collective-permute-start(bf16[2,1,2,1,256]{4,2,0,3,1:T(2,128)(2,1)S(1)} %bitcast.860), channel_id=1, source_target_pairs={{0,13},{1,12},{2,15},{3,14},{4,9},{5,8},{6,11},{7,10},{8,5},{9,4},... | collective-permute-start | bytes 6152 | tf_op jit(solution)/shard_map/ppermute | solution.py:31
  331.6 7.2 %collective-permute-start.29 = (bf16[2,1,2,1,256]{4,2,0,3,1:T(2,128)(2,1)S(1)}, bf16[2,1,2,1,256]{4,2,0,3,1:T(2,128)(2,1)S(1)}, u32[]{:S(2)}, u32[]{:S(2)}) collective-permute-start(bf16[2,1,2,1,256]{4,2,0,3,1:T(2,128)(2,1)S(1)} %bitcast.849), channel_id=1, source_target_pairs={{0,15},{1,14},{2,13},{3,12},{4,11},{5,10},{6,9},{7,8},{8,7},{9,6},... | collective-permute-start | bytes 6152 | tf_op jit(solution)/shard_map/ppermute | solution.py:31
  353.7 13.7 %all-to-all-start.9 = ((bf16[2,16,2,1,256]{4,2,0,3,1:T(2,128)(2,1)}), bf16[2,16,2,1,256]{4,2,0,3,1:T(2,128)(2,1)S(1)}, u32[]{:S(2)}, u32[]{:S(2)}) async-start(bf16[2,16,2,1,256]{4,2,0,3,1:T(2,128)(2,1)} %copy.358), calls=%async_computation.9 | async-start | bytes 65536 | tf_op jit(solution)/shard_map/all_to_all | solution.py:216
  360.0 184.4 %all-reduce.4.cloned.1.call-start = ((), (), s32[]{:S(2)}) async-start(), calls=%async_computation.10 | async-start | bytes 2752512 | tf_op jit(solution)/shard_map/psum | solution.py:221
  367.9 7.1 %collective-permute-start.30 = (bf16[2,1,2,1,256]{4,2,0,3,1:T(2,128)(2,1)S(1)}, bf16[2,1,2,1,256]{4,2,0,3,1:T(2,128)(2,1)S(1)}, u32[]{:S(2)}, u32[]{:S(2)}) collective-permute-start(bf16[2,1,2,1,256]{4,2,0,3,1:T(2,128)(2,1)S(1)} %bitcast.898), channel_id=1, source_target_pairs={{0,1},{1,0},{2,3},{3,2},{4,5},{5,4},{6,7},{7,6},{8,9},{9,8},{10,11... | collective-permute-start | bytes 6152 | tf_op jit(solution)/shard_map/ppermute | solution.py:31
  369.1 9.6 %collective-permute-start.32 = (bf16[2,1,2,1,256]{4,2,0,3,1:T(2,128)(2,1)S(1)}, bf16[2,1,2,1,256]{4,2,0,3,1:T(2,128)(2,1)S(1)}, u32[]{:S(2)}, u32[]{:S(2)}) collective-permute-start(bf16[2,1,2,1,256]{4,2,0,3,1:T(2,128)(2,1)S(1)} %bitcast.891), channel_id=1, source_target_pairs={{0,3},{1,2},{2,1},{3,0},{4,7},{5,6},{6,5},{7,4},{8,11},{9,10},{10,... | collective-permute-start | bytes 6152 | tf_op jit(solution)/shard_map/ppermute | solution.py:31
  371.5 8.0 %collective-permute-start.33 = (bf16[2,1,2,1,256]{4,2,0,3,1:T(2,128)(2,1)S(1)}, bf16[2,1,2,1,256]{4,2,0,3,1:T(2,128)(2,1)S(1)}, u32[]{:S(2)}, u32[]{:S(2)}) collective-permute-start(bf16[2,1,2,1,256]{4,2,0,3,1:T(2,128)(2,1)S(1)} %bitcast.880), channel_id=1, source_target_pairs={{0,4},{1,5},{2,6},{3,7},{4,0},{5,1},{6,2},{7,3},{8,12},{9,13},{10,... | collective-permute-start | bytes 6152 | tf_op jit(solution)/shard_map/ppermute | solution.py:31
  372.1 9.8 %collective-permute-start.34 = (bf16[2,1,2,1,256]{4,2,0,3,1:T(2,128)(2,1)S(1)}, bf16[2,1,2,1,256]{4,2,0,3,1:T(2,128)(2,1)S(1)}, u32[]{:S(2)}, u32[]{:S(2)}) collective-permute-start(bf16[2,1,2,1,256]{4,2,0,3,1:T(2,128)(2,1)S(1)} %bitcast.869), channel_id=1, source_target_pairs={{0,5},{1,4},{2,7},{3,6},{4,1},{5,0},{6,3},{7,2},{8,13},{9,12},{10,... | collective-permute-start | bytes 6152 | tf_op jit(solution)/shard_map/ppermute | solution.py:31
  375.0 8.6 %collective-permute-start.35 = (bf16[2,1,2,1,256]{4,2,0,3,1:T(2,128)(2,1)S(1)}, bf16[2,1,2,1,256]{4,2,0,3,1:T(2,128)(2,1)S(1)}, u32[]{:S(2)}, u32[]{:S(2)}) collective-permute-start(bf16[2,1,2,1,256]{4,2,0,3,1:T(2,128)(2,1)S(1)} %bitcast.893), channel_id=1, source_target_pairs={{0,6},{1,7},{2,4},{3,5},{4,2},{5,3},{6,0},{7,1},{8,14},{9,15},{10,... | collective-permute-start | bytes 6152 | tf_op jit(solution)/shard_map/ppermute | solution.py:31
  375.6 12.1 %collective-permute-start.36 = (bf16[2,1,2,1,256]{4,2,0,3,1:T(2,128)(2,1)S(1)}, bf16[2,1,2,1,256]{4,2,0,3,1:T(2,128)(2,1)S(1)}, u32[]{:S(2)}, u32[]{:S(2)}) collective-permute-start(bf16[2,1,2,1,256]{4,2,0,3,1:T(2,128)(2,1)S(1)} %bitcast.884), channel_id=1, source_target_pairs={{0,7},{1,6},{2,5},{3,4},{4,3},{5,2},{6,1},{7,0},{8,15},{9,14},{10,... | collective-permute-start | bytes 6152 | tf_op jit(solution)/shard_map/ppermute | solution.py:31
  378.8 9.6 %collective-permute-start.37 = (bf16[2,1,2,1,256]{4,2,0,3,1:T(2,128)(2,1)S(1)}, bf16[2,1,2,1,256]{4,2,0,3,1:T(2,128)(2,1)S(1)}, u32[]{:S(2)}, u32[]{:S(2)}) collective-permute-start(bf16[2,1,2,1,256]{4,2,0,3,1:T(2,128)(2,1)S(1)} %bitcast.871), channel_id=1, source_target_pairs={{0,8},{1,9},{2,10},{3,11},{4,12},{5,13},{6,14},{7,15},{8,0},{9,1},... | collective-permute-start | bytes 6152 | tf_op jit(solution)/shard_map/ppermute | solution.py:31
  379.4 12.2 %collective-permute-start.38 = (bf16[2,1,2,1,256]{4,2,0,3,1:T(2,128)(2,1)S(1)}, bf16[2,1,2,1,256]{4,2,0,3,1:T(2,128)(2,1)S(1)}, u32[]{:S(2)}, u32[]{:S(2)}) collective-permute-start(bf16[2,1,2,1,256]{4,2,0,3,1:T(2,128)(2,1)S(1)} %bitcast.864), channel_id=1, source_target_pairs={{0,9},{1,8},{2,11},{3,10},{4,13},{5,12},{6,15},{7,14},{8,1},{9,0},... | collective-permute-start | bytes 6152 | tf_op jit(solution)/shard_map/ppermute | solution.py:31
  381.9 10.4 %collective-permute-start.39 = (bf16[2,1,2,1,256]{4,2,0,3,1:T(2,128)(2,1)S(1)}, bf16[2,1,2,1,256]{4,2,0,3,1:T(2,128)(2,1)S(1)}, u32[]{:S(2)}, u32[]{:S(2)}) collective-permute-start(bf16[2,1,2,1,256]{4,2,0,3,1:T(2,128)(2,1)S(1)} %bitcast.856), channel_id=1, source_target_pairs={{0,10},{1,11},{2,8},{3,9},{4,14},{5,15},{6,12},{7,13},{8,2},{9,3},... | collective-permute-start | bytes 6152 | tf_op jit(solution)/shard_map/ppermute | solution.py:31
  383.6 13.8 %collective-permute-start.40 = (bf16[2,1,2,1,256]{4,2,0,3,1:T(2,128)(2,1)S(1)}, bf16[2,1,2,1,256]{4,2,0,3,1:T(2,128)(2,1)S(1)}, u32[]{:S(2)}, u32[]{:S(2)}) collective-permute-start(bf16[2,1,2,1,256]{4,2,0,3,1:T(2,128)(2,1)S(1)} %bitcast.872), channel_id=1, source_target_pairs={{0,11},{1,10},{2,9},{3,8},{4,15},{5,14},{6,13},{7,12},{8,3},{9,2},... | collective-permute-start | bytes 6152 | tf_op jit(solution)/shard_map/ppermute | solution.py:31
  387.7 9.7 %collective-permute-start.41 = (bf16[2,1,2,1,256]{4,2,0,3,1:T(2,128)(2,1)S(1)}, bf16[2,1,2,1,256]{4,2,0,3,1:T(2,128)(2,1)S(1)}, u32[]{:S(2)}, u32[]{:S(2)}) collective-permute-start(bf16[2,1,2,1,256]{4,2,0,3,1:T(2,128)(2,1)S(1)} %bitcast.865), channel_id=1, source_target_pairs={{0,12},{1,13},{2,14},{3,15},{4,8},{5,9},{6,10},{7,11},{8,4},{9,5},... | collective-permute-start | bytes 6152 | tf_op jit(solution)/shard_map/ppermute | solution.py:31
  388.4 9.0 %collective-permute-start.42 = (bf16[2,1,2,1,256]{4,2,0,3,1:T(2,128)(2,1)S(1)}, bf16[2,1,2,1,256]{4,2,0,3,1:T(2,128)(2,1)S(1)}, u32[]{:S(2)}, u32[]{:S(2)}) collective-permute-start(bf16[2,1,2,1,256]{4,2,0,3,1:T(2,128)(2,1)S(1)} %bitcast.859), channel_id=1, source_target_pairs={{0,13},{1,12},{2,15},{3,14},{4,9},{5,8},{6,11},{7,10},{8,5},{9,4},... | collective-permute-start | bytes 6152 | tf_op jit(solution)/shard_map/ppermute | solution.py:31
  392.3 7.2 %collective-permute-start.44 = (bf16[2,1,2,1,256]{4,2,0,3,1:T(2,128)(2,1)S(1)}, bf16[2,1,2,1,256]{4,2,0,3,1:T(2,128)(2,1)S(1)}, u32[]{:S(2)}, u32[]{:S(2)}) collective-permute-start(bf16[2,1,2,1,256]{4,2,0,3,1:T(2,128)(2,1)S(1)} %bitcast.847), channel_id=1, source_target_pairs={{0,15},{1,14},{2,13},{3,12},{4,11},{5,10},{6,9},{7,8},{8,7},{9,6},... | collective-permute-start | bytes 6152 | tf_op jit(solution)/shard_map/ppermute | solution.py:31
  (167 other events, 860.4 us)
Sparse Core Ops, SparseCore 0:
  411.1 133.2 all-reduce.3
